TPU v7x, 128 devices: a whole 4x4x4 slice. The times are simulated.
128 devices in a mesh: patch: 16 (over z, x_lo, core), head: 8 (over y, x_hi).
Axes of the slice: x: 4 (x_hi: 2, x_lo: 2; x = x_hi * 2 + x_lo), y: 4, z: 4, core: 2. Of those that a mesh axis runs over, the one named last changes fastest.
Arguments:
- img_qkv: bfloat16 [8192, 9216], P(('patch', 'head')), may hold values from -8 to 8
- txt_qkv: bfloat16 [512, 9216], P('head'), may hold values from -8 to 8
- stale_kv: bfloat16 [2, 8192, 3072], P(None, 'patch', 'head'), may hold values from -8 to 8
- residual: bfloat16 [8192, 3072], P(('patch', 'head')), may hold values from -4 to 4
- gate_scale: float32 [3072], replicated, may hold values from 0.5 to 3
- proj_weight: bfloat16 [3072, 3072], replicated, may hold values from -0.109375 to 0.109375
Outputs:
- image_out: bfloat16 [8192, 3072], P(('patch', 'head'))
- text_attn: bfloat16 [512, 3072], P('head')
All inputs are finite; a program needn't handle non-finite values.
Results may differ from a plain program's by a relative error of at most 0.0075.
Values may be sent and summed in bfloat16 or wider, within the bound.
A program may use at most 192 MiB of HBM per device.

v0:
```python
import math
import jax
import jax.numpy as jnp
from jax import lax
from jax.sharding import PartitionSpec as P

HD = 128


def block_stats(queries, key_rows, values):
    scores = jnp.einsum("rhd,khd->rhk", queries, key_rows, preferred_element_type=jnp.float32) * (
        1.0 / math.sqrt(HD)
    )
    row_max = jnp.max(scores, axis=2)
    shifted = jnp.exp(scores - row_max[:, :, None])
    row_sum = jnp.sum(shifted, axis=2)
    weighted = jnp.einsum(
        "rhk,khd->rhd", shifted.astype(jnp.bfloat16), values, preferred_element_type=jnp.float32
    )
    return (row_max, row_sum, weighted)


def combine(first, second):
    joint_max = jnp.maximum(first[0], second[0])
    first_scale = jnp.exp(first[0] - joint_max)
    second_scale = jnp.exp(second[0] - joint_max)
    return (
        joint_max,
        first[1] * first_scale + second[1] * second_scale,
        first[2] * first_scale[:, :, None] + second[2] * second_scale[:, :, None],
    )


def finish(totals):
    return (totals[2] / totals[1][:, :, None]).astype(jnp.bfloat16)


def per_device(img_qkv, txt_qkv, stale_kv, residual, gate_scale, proj_weight):
    my_group = lax.axis_index("patch")
    img_rows = img_qkv.shape[0]
    model_width = img_qkv.shape[1] // 3
    head_count = model_width // HD
    img_split = img_qkv.reshape(img_rows, 3, head_count, HD)
    txt_split = txt_qkv.reshape(txt_qkv.shape[0], 3, head_count, HD)
    img_heads, txt_heads = (
        lax.all_to_all(img_split, "head", split_axis=2, concat_axis=0, tiled=True),
        lax.all_to_all(txt_split, "head", split_axis=2, concat_axis=0, tiled=True),
    )
    query_img = img_heads[:, 0]
    keys_img = img_heads[:, 1]
    values_img = img_heads[:, 2]
    query_txt = txt_heads[:, 0]
    keys_txt = txt_heads[:, 1]
    values_txt = txt_heads[:, 2]
    group_rows = query_img.shape[0]
    local_heads = query_img.shape[1]
    image_init = block_stats(query_img, keys_txt, values_txt)
    text_init = block_stats(query_txt, keys_txt, values_txt)
    own_first = my_group * group_rows
    shard_rows = lax.all_gather(stale_kv, "patch", axis=1, tiled=True)
    shard_count = shard_rows.shape[1] // group_rows
    key_blocks = jnp.moveaxis(shard_rows.reshape(2, shard_count, group_rows, local_heads, HD), 1, 0)
    starts = group_rows * jnp.arange(shard_count, dtype=jnp.int32)

    def one_block(running_pair, inputs):
        key_block, block_first = inputs
        is_fresh = block_first == own_first
        key_rows = jnp.where(is_fresh, keys_img, key_block[0])
        values = jnp.where(is_fresh, values_img, key_block[1])
        image_next = combine(running_pair[0], block_stats(query_img, key_rows, values))
        text_next = combine(running_pair[1], block_stats(query_txt, key_block[0], key_block[1]))
        return ((image_next, text_next), None)

    result, _ = lax.scan(one_block, (image_init, text_init), (key_blocks, starts))
    image_total, text_total = result
    image_attn = finish(image_total)
    text_attn = finish(text_total)
    image_back, text_back = (
        lax.all_to_all(image_attn, "head", split_axis=0, concat_axis=1, tiled=True),
        lax.all_to_all(text_attn, "head", split_axis=0, concat_axis=1, tiled=True),
    )
    image_flat = image_back.reshape(img_rows, model_width)
    projected = jnp.dot(image_flat, proj_weight, preferred_element_type=jnp.float32)
    image_out = (residual.astype(jnp.float32) + gate_scale * projected).astype(jnp.bfloat16)
    return (image_out, text_back.reshape(text_back.shape[0], model_width))


def solution(mesh):
    return jax.shard_map(
        per_device,
        mesh=mesh,
        in_specs=(
            P(("patch", "head"), None),
            P("head", None),
            P(None, "patch", "head"),
            P(("patch", "head"), None),
            P(),
            P(),
        ),
        out_specs=(P(("patch", "head"), None), P("head", None)),
        check_vma=False,
    )
```

profile of v0, /device:TPU:96, one launch (start us, length us, event | category | flops | bytes accessed | tf_op | source)
XLA Modules:
  0.0 355.6 jit_solution(2656296785264345013)
XLA Ops:
  10.8 6.9 %all-to-all-start.1 = ((bf16[64,3,24,128]{3,0,1,2:T(8,128)(2,1)}), bf16[64,3,24,128]{3,0,1,2:T(8,128)(2,1)S(1)}, u32[]{:S(2)}, u32[]{:S(2)}) async-start(bf16[64,3,24,128]{3,0,1,2:T(8,128)(2,1)} %copy.82), calls=%async_computation.1 | async-start | bytes 2359296 | tf_op jit(solution)/shard_map/all_to_all | solution.py:46
  19.3 29.1 %all-to-all-done.1 = bf16[64,3,24,128]{3,0,1,2:T(8,128)(2,1)S(1)} async-done(((bf16[64,3,24,128]{3,0,1,2:T(8,128)(2,1)}), bf16[64,3,24,128]{3,0,1,2:T(8,128)(2,1)S(1)}, u32[]{:S(2)}, u32[]{:S(2)}) %all-to-all-start.1) | async-done | bytes 1179680 | tf_op jit(solution)/shard_map/all_to_all | solution.py:46
  48.3 4.3 %all-to-all-start = ((bf16[64,3,24,128]{3,0,1,2:T(8,128)(2,1)}), bf16[64,3,24,128]{3,0,1,2:T(8,128)(2,1)}, u32[]{:S(2)}, u32[]{:S(2)}) async-start(bf16[64,3,24,128]{3,0,1,2:T(8,128)(2,1)} %copy.79), calls=%async_computation | async-start | bytes 2359296 | tf_op jit(solution)/shard_map/all_to_all | solution.py:47
  52.7 30.9 %all-to-all-done = bf16[64,3,24,128]{3,0,1,2:T(8,128)(2,1)} async-done(((bf16[64,3,24,128]{3,0,1,2:T(8,128)(2,1)}), bf16[64,3,24,128]{3,0,1,2:T(8,128)(2,1)}, u32[]{:S(2)}, u32[]{:S(2)}) %all-to-all-start) | async-done | bytes 1179680 | tf_op jit(solution)/shard_map/all_to_all | solution.py:47
  94.2 2.9 fusion.49
  97.2 7.7 %all-gather.2.cloned.1.call-done = bf16[2,8192,384]{2,1,0:T(8,128)(2,1)} async-done(((bf16[2,512,384]{2,1,0:T(8,128)(2,1)}), bf16[2,8192,384]{2,1,0:T(8,128)(2,1)}) %all-gather.2.cloned.1.call-update) | async-done | bytes 12582928 | tf_op jit(solution)/shard_map/all_gather | solution.py:60
  104.9 16.7 %copy.87 = bf16[2,8192,384]{1,2,0:T(8,128)(2,1)} copy(bf16[2,8192,384]{2,1,0:T(8,128)(2,1)} %all-gather.2.cloned.1.call-done) | data formatting | bytes 25165824 | tf_op jit(solution)/shard_map/all_gather | solution.py:60
  121.6 12.8 %copy.109 = bf16[96,8,16,512]{3,2,1,0:T(8,128)(2,1)} copy(bf16[96,8,16,512]{3,1,2,0:T(8,128)(2,1)} %bitcast.177) | data formatting | bytes 25165824
  134.4 17.5 %copy.90 = bf16[16,2,512,3,128]{4,2,3,1,0:T(8,128)(2,1)} copy(bf16[16,2,512,3,128]{2,0,4,3,1:T(8,128)(2,1)} %bitcast.178) | data formatting | bytes 25165824 | tf_op jit(solution)/shard_map/while | solution.py:74
  152.0 149.5 %while.20 = (s32[]{:T(128)}, f32[512,3]{0,1:T(4,128)S(1)}, f32[512,3]{0,1:T(4,128)S(1)}, f32[512,3,128]{0,2,1:T(8,128)S(1)}, f32[512,3]{0,1:T(4,128)S(1)}, /*ind...) while((s32[]{:T(128)}, f32[512,3]{0,1:T(4,128)S(1)}, ...), condition=%wide.region_9.10_spmd, body=%wide.region_4.9_spmd.sunk | while | flops 819474432 | bytes 25338080 | solution.py:74
  168.8 1.9 fusion.90
  178.1 1.9 fusion.90
  187.4 1.9 fusion.90
  196.8 1.9 fusion.90
  206.1 1.9 fusion.90
  215.5 1.9 fusion.90
  224.8 1.9 fusion.90
  234.2 1.9 fusion.90
  243.5 1.9 fusion.90
  303.4 7.5 %all-to-all-start.3 = ((bf16[512,3,128]{2,1,0:T(4,128)(2,1)}), bf16[512,3,128]{2,1,0:T(4,128)(2,1)S(1)}, u32[]{:S(2)}, u32[]{:S(2)}) async-start(bf16[512,3,128]{2,1,0:T(4,128)(2,1)} %divide_convert_fusion), calls=%async_computation.3 | async-start | bytes 1048576 | tf_op jit(solution)/shard_map/all_to_all | solution.py:80
  312.9 10.0 %all-to-all-done.3 = bf16[512,3,128]{2,1,0:T(4,128)(2,1)S(1)} async-done(((bf16[512,3,128]{2,1,0:T(4,128)(2,1)}), bf16[512,3,128]{2,1,0:T(4,128)(2,1)S(1)}, u32[]{:S(2)}, u32[]{:S(2)}) %all-to-all-start.3) | async-done | bytes 393248 | tf_op jit(solution)/shard_map/all_to_all | solution.py:80
  323.0 3.7 %all-to-all-start.2 = ((bf16[512,3,128]{2,1,0:T(4,128)(2,1)}), bf16[512,3,128]{2,1,0:T(4,128)(2,1)S(1)}, u32[]{:S(2)}, u32[]{:S(2)}) async-start(bf16[512,3,128]{2,1,0:T(4,128)(2,1)} %divide_convert_fusion.1), calls=%async_computation.2 | async-start | bytes 1048576 | tf_op jit(solution)/shard_map/all_to_all | solution.py:79
  328.1 9.3 %all-to-all-done.2 = bf16[512,3,128]{2,1,0:T(4,128)(2,1)S(1)} async-done(((bf16[512,3,128]{2,1,0:T(4,128)(2,1)}), bf16[512,3,128]{2,1,0:T(4,128)(2,1)S(1)}, u32[]{:S(2)}, u32[]{:S(2)}) %all-to-all-start.2) | async-done | bytes 393248 | tf_op jit(solution)/shard_map/all_to_all | solution.py:79
  338.2 10.5 %fusion.45 = bf16[64,3072]{1,0:T(8,128)(2,1)} fusion(bf16[64,3072]{1,0:T(8,128)(2,1)S(1)} %reshape.39, bf16[3072,3072]{1,0:T(8,128)(2,1)} %param.13, bf16[64,3072]{1,0:T(8,128)(2,1)S(1)} %copy-done.6, f32[3072]{0:T(1024)S(1)} %copy-done.7), kind=kOutput, calls=%fused_computation.44 | convolution fusion | flops 1208745984 | bytes 20066304 | tf_op jit(solution)/shard_map/dot_general | solution.py:83
  (163 shorter events, 143.5 us)
Async XLA Ops:
  7.2 97.8 %all-gather.2.cloned.1.call-start = ((), (), s32[]{:S(2)}) async-start(), calls=%async_computation.4 | async-start | bytes 13369344 | tf_op jit(solution)/shard_map/all_gather | solution.py:60
  7.9 9.8 %copy-start.5 = (bf16[64,9216]{1,0:T(8,128)(2,1)S(1)}, bf16[64,9216]{1,0:T(8,128)(2,1)}, u32[]{:S(2)}) copy-start(bf16[64,9216]{1,0:T(8,128)(2,1)} %param.9) | copy-start | bytes 3538948
  10.8 37.5 %all-to-all-start.1 = ((bf16[64,3,24,128]{3,0,1,2:T(8,128)(2,1)}), bf16[64,3,24,128]{3,0,1,2:T(8,128)(2,1)S(1)}, u32[]{:S(2)}, u32[]{:S(2)}) async-start(bf16[64,3,24,128]{3,0,1,2:T(8,128)(2,1)} %copy.82), calls=%async_computation.1 | async-start | bytes 2359296 | tf_op jit(solution)/shard_map/all_to_all | solution.py:46
  48.3 35.3 %all-to-all-start = ((bf16[64,3,24,128]{3,0,1,2:T(8,128)(2,1)}), bf16[64,3,24,128]{3,0,1,2:T(8,128)(2,1)}, u32[]{:S(2)}, u32[]{:S(2)}) async-start(bf16[64,3,24,128]{3,0,1,2:T(8,128)(2,1)} %copy.79), calls=%async_computation | async-start | bytes 2359296 | tf_op jit(solution)/shard_map/all_to_all | solution.py:47
  52.7 32.9 %copy-start.4 = (bf16[8,64,3,3,128]{4,1,0,3,2:T(8,128)(2,1)}, bf16[8,64,3,3,128]{4,1,0,3,2:T(8,128)(2,1)S(1)}, u32[]{:S(2)}) copy-start(bf16[8,64,3,3,128]{4,1,0,3,2:T(8,128)(2,1)S(1)} %copy.84) | copy-start | bytes 3538948
  85.0 4.0 %copy-start.3 = (bf16[8,64,3,3,128]{4,1,0,3,2:T(8,128)(2,1)}, bf16[8,64,3,3,128]{4,1,0,3,2:T(8,128)(2,1)S(1)}, u32[]{:S(2)}) copy-start(bf16[8,64,3,3,128]{4,1,0,3,2:T(8,128)(2,1)S(1)} %copy.81) | copy-start | bytes 3538948
  85.6 1.6 copy-start
  89.0 1.6 copy-start.2
  91.8 2.5 copy-start.1
  303.4 19.5 %all-to-all-start.3 = ((bf16[512,3,128]{2,1,0:T(4,128)(2,1)}), bf16[512,3,128]{2,1,0:T(4,128)(2,1)S(1)}, u32[]{:S(2)}, u32[]{:S(2)}) async-start(bf16[512,3,128]{2,1,0:T(4,128)(2,1)} %divide_convert_fusion), calls=%async_computation.3 | async-start | bytes 1048576 | tf_op jit(solution)/shard_map/all_to_all | solution.py:80
  312.9 25.3 %copy-start.6 = (bf16[64,3072]{1,0:T(8,128)(2,1)S(1)}, bf16[64,3072]{1,0:T(8,128)(2,1)}, u32[]{:S(2)}) copy-start(bf16[64,3072]{1,0:T(8,128)(2,1)} %param.11) | copy-start | bytes 1179652
  312.9 25.3 %copy-start.7 = (f32[3072]{0:T(1024)S(1)}, f32[3072]{0:T(1024)}, u32[]{:S(2)}) copy-start(f32[3072]{0:T(1024)} %param.12) | copy-start | bytes 36868
  323.0 14.5 %all-to-all-start.2 = ((bf16[512,3,128]{2,1,0:T(4,128)(2,1)}), bf16[512,3,128]{2,1,0:T(4,128)(2,1)S(1)}, u32[]{:S(2)}, u32[]{:S(2)}) async-start(bf16[512,3,128]{2,1,0:T(4,128)(2,1)} %divide_convert_fusion.1), calls=%async_computation.2 | async-start | bytes 1048576 | tf_op jit(solution)/shard_map/all_to_all | solution.py:79
Sparse Core Ops, SparseCore 0:
  9.6 95.2 all-gather.1
where the time goes:
time: 360 us; the launch traced here: 356 us
  matrix products  125 us (35%)
  waiting for transfers between devices  87.7 us (24%)
  local copies, waits for them, and re-layouts  72.4 us (20%)
  other arithmetic  23.4 us (6%)
  starting transfers between devices  22.4 us (6%)
  between operations  14.3 us (4%)
  loops' own time  10.8 us (3%)
    dot_general x34, matrix products, block_stats(): jnp.einsum('rhk,khd->rhd', shifted.astype(jnp.bfloat16), values, preferre...  62.2 us
    dot_general x34, matrix products, block_stats(): jnp.einsum('rhd,khd->rhk', queries, key_rows, preferred_element_type=jnp....  51.9 us
    all_to_all x1, waiting for transfers between devices, per_device(): lax.all_to_all(txt_split, 'head', split_axis=2, concat_axis=0, tiled=True)  30.9 us
    all_to_all x1, waiting for transfers between devices, per_device(): lax.all_to_all(img_split, 'head', split_axis=2, concat_axis=0, tiled=True)  29.1 us
    reduce_sum x33, other arithmetic, block_stats(): row_sum = jnp.sum(shifted, axis=2)  20 us
    while x7, local copies, waits for them, and re-layouts, per_device(): lax.scan(one_block, (image_init, text_init), (key_blocks, starts))  19.1 us
    unnamed x19, local copies, waits for them, and re-layouts  18.7 us
    all_gather x1, local copies, waits for them, and re-layouts, per_device(): shard_rows = lax.all_gather(stale_kv, 'patch', axis=1, tiled=True)  16.7 us
  transfers between devices with their start and end apart: 5, of which 5 were waited for; matrix products, arithmetic and copies ran while one was open for 5% of the time, Pallas kernels for 0%

commit v1 on v0

--- a/solution.py
+++ b/solution.py
@@ -57,7 +57,9 @@
     image_init = block_stats(query_img, keys_txt, values_txt)
     text_init = block_stats(query_txt, keys_txt, values_txt)
     own_first = my_group * group_rows
-    shard_rows = lax.all_gather(stale_kv, "patch", axis=1, tiled=True)
+    shard_rows = jnp.concatenate(
+        lax.all_to_all(jnp.stack([stale_kv] * lax.axis_size("patch")), "patch", 0, 0), axis=1
+    )
     shard_count = shard_rows.shape[1] // group_rows
     key_blocks = jnp.moveaxis(shard_rows.reshape(2, shard_count, group_rows, local_heads, HD), 1, 0)
     starts = group_rows * jnp.arange(shard_count, dtype=jnp.int32)

time: 360 us -> 481 us (1.34)
  waiting for transfers between devices: 87.7 us -> 168 us
  local copies, waits for them, and re-layouts: 72.4 us -> 110 us
  other arithmetic: 23.4 us -> 44 us
  between operations: 14.3 us -> 0.84 us
  matrix products: 125 us -> 118 us
    all_to_all x0 -> x1, waiting for transfers between devices: none -> 116 us  [per_device(): lax.all_to_all(jnp.stack([stale_kv] * lax.axis_size('patch')), 'patch', 0...]
    while x0 -> x320, local copies, waits for them, and re-layouts: none -> 45.1 us
    add x16, other arithmetic: 0.58 us -> 21.2 us  [combine(): first[1] * first_scale + second[1] * second_scale]
    slice x0 -> x16, local copies, waits for them, and re-layouts: none -> 18.6 us  [one_block(): values = jnp.where(is_fresh, values_img, key_block[1])]
    all_gather x1 -> x0, local copies, waits for them, and re-layouts: 16.7 us -> none  [per_device(): shard_rows = lax.all_gather(stale_kv, 'patch', axis=1, tiled=True)]
    all_to_all x1, waiting for transfers between devices: 30.9 us -> 17.1 us  [per_device(): lax.all_to_all(txt_split, 'head', split_axis=2, concat_axis=0, tiled=True)]
    unnamed x19 -> x21, local copies, waits for them, and re-layouts: 18.7 us -> 6.03 us
    all_to_all x1, waiting for transfers between devices: 29.1 us -> 16.5 us  [per_device(): lax.all_to_all(img_split, 'head', split_axis=2, concat_axis=0, tiled=True)]
where the time goes in v1:
time: 481 us; the launch traced here: 475 us
  waiting for transfers between devices  168 us (35%)
  matrix products  118 us (25%)
  local copies, waits for them, and re-layouts  110 us (23%)
  other arithmetic  44 us (9%)
  starting transfers between devices  22.7 us (5%)
  loops' own time  11.1 us (2%)
    all_to_all x1, waiting for transfers between devices, per_device(): lax.all_to_all(jnp.stack([stale_kv] * lax.axis_size('patch')), 'patch', 0...  116 us
    dot_general x34, matrix products, block_stats(): jnp.einsum('rhk,khd->rhd', shifted.astype(jnp.bfloat16), values, preferre...  65.7 us
    while x320, local copies, waits for them, and re-layouts  45.1 us
    dot_general x34, matrix products, block_stats(): jnp.einsum('rhd,khd->rhk', queries, key_rows, preferred_element_type=jnp....  42.2 us
    add x16, other arithmetic, combine(): first[1] * first_scale + second[1] * second_scale  21.2 us
    reduce_sum x33, other arithmetic, block_stats(): row_sum = jnp.sum(shifted, axis=2)  19.4 us
    dynamic_slice x16, local copies, waits for them, and re-layouts, per_device(): lax.scan(one_block, (image_init, text_init), (key_blocks, starts))  18.9 us
    slice x16, local copies, waits for them, and re-layouts, one_block(): values = jnp.where(is_fresh, values_img, key_block[1])  18.6 us
  transfers between devices with their start and end apart: 5, of which 5 were waited for; matrix products, arithmetic and copies ran while one was open for 5% of the time, Pallas kernels for 0%

profile of v1, /device:TPU:96, one launch (start us, length us, event | category | flops | bytes accessed | tf_op | source)
XLA Modules:
  0.0 475.0 jit_solution(3436450128798746405)
XLA Ops:
  3.5 6.9 %all-to-all-start = ((bf16[64,3,24,128]{3,0,1,2:T(8,128)(2,1)}), bf16[64,3,24,128]{3,0,1,2:T(8,128)(2,1)S(1)}, u32[]{:S(2)}, u32[]{:S(2)}) async-start(bf16[64,3,24,128]{3,0,1,2:T(8,128)(2,1)} %copy.80), calls=%async_computation | async-start | bytes 2359296 | tf_op jit(solution)/shard_map/all_to_all | solution.py:47
  12.0 17.1 %all-to-all-done = bf16[64,3,24,128]{3,0,1,2:T(8,128)(2,1)S(1)} async-done(((bf16[64,3,24,128]{3,0,1,2:T(8,128)(2,1)}), bf16[64,3,24,128]{3,0,1,2:T(8,128)(2,1)S(1)}, u32[]{:S(2)}, u32[]{:S(2)}) %all-to-all-start) | async-done | bytes 1179680 | tf_op jit(solution)/shard_map/all_to_all | solution.py:47
  29.1 3.6 all-to-all-start.1
  34.1 16.5 %all-to-all-done.1 = bf16[64,3,24,128]{3,0,1,2:T(8,128)(2,1)S(1)} async-done(((bf16[64,3,24,128]{3,0,1,2:T(8,128)(2,1)}), bf16[64,3,24,128]{3,0,1,2:T(8,128)(2,1)S(1)}, u32[]{:S(2)}, u32[]{:S(2)}) %all-to-all-start.1) | async-done | bytes 1179680 | tf_op jit(solution)/shard_map/all_to_all | solution.py:46
  50.6 5.9 %stack.2 = bf16[16,2,512,384]{2,3,1,0:T(8,128)(2,1)} broadcast(bf16[2,512,384]{1,2,0:T(8,128)(2,1)S(1)} %copy.88), dimensions={1,2,3} | broadcast | bytes 13369344 | tf_op jit(solution)/shard_map/stack | solution.py:61
  56.5 5.0 %all-to-all-start.2 = ((bf16[16,2,512,384]{2,3,1,0:T(8,128)(2,1)}), bf16[16,2,512,384]{2,3,1,0:T(8,128)(2,1)}, u32[]{:S(2)}, u32[]{:S(2)}) async-start(bf16[16,2,512,384]{2,3,1,0:T(8,128)(2,1)} %stack.2), calls=%async_computation.2 | async-start | bytes 25165824 | tf_op jit(solution)/shard_map/all_to_all | solution.py:61
  83.6 116.1 %all-to-all-done.2 = bf16[16,2,512,384]{2,3,1,0:T(8,128)(2,1)} async-done(((bf16[16,2,512,384]{2,3,1,0:T(8,128)(2,1)}), bf16[16,2,512,384]{2,3,1,0:T(8,128)(2,1)}, u32[]{:S(2)}, u32[]{:S(2)}) %all-to-all-start.2) | async-done | bytes 12582944 | tf_op jit(solution)/shard_map/all_to_all | solution.py:61
  199.7 231.0 %while.20 = (s32[]{:T(128)}, f32[512,3]{0,1:T(4,128)}, f32[512,3]{0,1:T(4,128)}, f32[512,3,128]{0,2,1:T(8,128)}, f32[512,3]{0,1:T(4,128)}, /*index=5*/f32[512,3]...) while((s32[]{:T(128)}, f32[512,3]{0,1:T(4,128)}, ...), condition=%wide.region_9.10_spmd, body=%wide.region_4.9_spmd.sunk | while | flops 819474432 | bytes 39592388 | solution.py:76
  211.3 2.9 fusion.86
  225.7 2.9 fusion.86
  240.1 2.9 fusion.86
  254.5 2.9 fusion.86
  269.0 2.9 fusion.86
  283.4 2.9 fusion.86
  297.8 2.9 fusion.86
  312.2 2.9 fusion.86
  326.7 2.9 fusion.86
  341.1 2.9 fusion.86
  384.5 3.0 fusion.86
  434.6 3.5 all-to-all-start.4
  440.1 9.5 %all-to-all-done.4 = bf16[512,3,128]{2,1,0:T(4,128)(2,1)S(1)} async-done(((bf16[512,3,128]{2,1,0:T(4,128)(2,1)}), bf16[512,3,128]{2,1,0:T(4,128)(2,1)S(1)}, u32[]{:S(2)}, u32[]{:S(2)}) %all-to-all-start.4) | async-done | bytes 393248 | tf_op jit(solution)/shard_map/all_to_all | solution.py:82
  449.6 3.7 all-to-all-start.3
  454.8 8.9 %all-to-all-done.3 = bf16[512,3,128]{2,1,0:T(4,128)(2,1)S(1)} async-done(((bf16[512,3,128]{2,1,0:T(4,128)(2,1)}), bf16[512,3,128]{2,1,0:T(4,128)(2,1)S(1)}, u32[]{:S(2)}, u32[]{:S(2)}) %all-to-all-start.3) | async-done | bytes 393248 | tf_op jit(solution)/shard_map/all_to_all | solution.py:81
  464.5 10.5 %fusion.41 = bf16[64,3072]{1,0:T(8,128)(2,1)} fusion(bf16[64,3072]{1,0:T(8,128)(2,1)S(1)} %reshape.41, bf16[3072,3072]{1,0:T(8,128)(2,1)} %param.13, bf16[64,3072]{1,0:T(8,128)(2,1)S(1)} %copy-done.16, f32[3072]{0:T(1024)S(1)} %copy-done.17), kind=kOutput, calls=%fused_computation.42 | convolution fusion | flops 1208745984 | bytes 20066304 | tf_op jit(solution)/shard_map/dot_general | solution.py:85
  (499 shorter events, 224.2 us)
Async XLA Ops:
  0.6 9.8 %copy-start.10 = (bf16[64,9216]{1,0:T(8,128)(2,1)S(1)}, bf16[64,9216]{1,0:T(8,128)(2,1)}, u32[]{:S(2)}) copy-start(bf16[64,9216]{1,0:T(8,128)(2,1)} %param.8) | copy-start | bytes 3538948
  3.5 25.6 %all-to-all-start = ((bf16[64,3,24,128]{3,0,1,2:T(8,128)(2,1)}), bf16[64,3,24,128]{3,0,1,2:T(8,128)(2,1)S(1)}, u32[]{:S(2)}, u32[]{:S(2)}) async-start(bf16[64,3,24,128]{3,0,1,2:T(8,128)(2,1)} %copy.80), calls=%async_computation | async-start | bytes 2359296 | tf_op jit(solution)/shard_map/all_to_all | solution.py:47
  29.1 21.5 %all-to-all-start.1 = ((bf16[64,3,24,128]{3,0,1,2:T(8,128)(2,1)}), bf16[64,3,24,128]{3,0,1,2:T(8,128)(2,1)S(1)}, u32[]{:S(2)}, u32[]{:S(2)}) async-start(bf16[64,3,24,128]{3,0,1,2:T(8,128)(2,1)} %copy.83), calls=%async_computation.1 | async-start | bytes 2359296 | tf_op jit(solution)/shard_map/all_to_all | solution.py:46
  56.5 143.2 %all-to-all-start.2 = ((bf16[16,2,512,384]{2,3,1,0:T(8,128)(2,1)}), bf16[16,2,512,384]{2,3,1,0:T(8,128)(2,1)}, u32[]{:S(2)}, u32[]{:S(2)}) async-start(bf16[16,2,512,384]{2,3,1,0:T(8,128)(2,1)} %stack.2), calls=%async_computation.2 | async-start | bytes 25165824 | tf_op jit(solution)/shard_map/all_to_all | solution.py:61
  200.9 2.7 copy-start
  215.3 2.7 copy-start
  229.7 2.7 copy-start
  244.1 2.7 copy-start
  258.6 2.7 copy-start
  287.4 2.7 copy-start
  301.8 2.7 copy-start
  316.3 2.7 copy-start
  330.7 2.7 copy-start
  345.1 2.7 copy-start
  359.5 2.7 copy-start
  374.0 2.7 copy-start
  388.6 2.7 copy-start
  403.0 2.7 copy-start
  430.7 7.4 %copy-start.4 = (f32[512,3,128]{0,2,1:T(8,128)S(1)}, f32[512,3,128]{0,2,1:T(8,128)}, u32[]{:S(2)}) copy-start(f32[512,3,128]{0,2,1:T(8,128)} %get-tuple-element.77) | copy-start | bytes 2359300
  430.7 7.8 %copy-start.13 = (f32[512,3]{0,1:T(4,128)S(1)}, f32[512,3]{0,1:T(4,128)}, u32[]{:S(2)}) copy-start(f32[512,3]{0,1:T(4,128)} %get-tuple-element.78) | copy-start | bytes 18436
  434.6 15.0 %all-to-all-start.4 = ((bf16[512,3,128]{2,1,0:T(4,128)(2,1)}), bf16[512,3,128]{2,1,0:T(4,128)(2,1)S(1)}, u32[]{:S(2)}, u32[]{:S(2)}) async-start(bf16[512,3,128]{2,1,0:T(4,128)(2,1)} %divide_convert_fusion), calls=%async_computation.4 | async-start | bytes 1048576 | tf_op jit(solution)/shard_map/all_to_all | solution.py:82
  440.1 24.4 %copy-start.16 = (bf16[64,3072]{1,0:T(8,128)(2,1)S(1)}, bf16[64,3072]{1,0:T(8,128)(2,1)}, u32[]{:S(2)}) copy-start(bf16[64,3072]{1,0:T(8,128)(2,1)} %param.11) | copy-start | bytes 1179652
  440.1 24.4 %copy-start.17 = (f32[3072]{0:T(1024)S(1)}, f32[3072]{0:T(1024)}, u32[]{:S(2)}) copy-start(f32[3072]{0:T(1024)} %param.12) | copy-start | bytes 36868
  449.6 14.2 %all-to-all-start.3 = ((bf16[512,3,128]{2,1,0:T(4,128)(2,1)}), bf16[512,3,128]{2,1,0:T(4,128)(2,1)S(1)}, u32[]{:S(2)}, u32[]{:S(2)}) async-start(bf16[512,3,128]{2,1,0:T(4,128)(2,1)} %divide_convert_fusion.1), calls=%async_computation.3 | async-start | bytes 1048576 | tf_op jit(solution)/shard_map/all_to_all | solution.py:81
  (134 other events, 239.8 us)
